TPU v7x, 32 devices: a whole 2x2x4 slice. The times are simulated.
32 devices in a mesh: dp: 4 (over x, core), ctx: 2 (over y), tensor: 4 (over z).
Axes of the slice: x: 2, y: 2, z: 4, core: 2. Of those that a mesh axis runs over, the one named last changes fastest.
Arguments:
- inputs: bfloat16 [2048, 2048], P(('dp', 'ctx'), 'tensor'), may hold values from -6 to 6
- cotangent: bfloat16 [2048, 2048], P(('dp', 'ctx')), may hold values from -6 to 6
- segments: int32 [4, 512], P('dp'), may hold values from 0 to 15, as said below
- positions: int32 [4, 512], P('dp', 'ctx'), may hold values from 0 to 511, as said below
- attention_gain: bfloat16 [2048], replicated, may hold values from 0.5 to 1.5
- query_weight: bfloat16 [2048, 2048], P(None, 'tensor'), may hold values from -0.125 to 0.125
- key_weight: bfloat16 [2048, 1024], P(None, 'tensor'), may hold values from -0.125 to 0.125
- value_weight: bfloat16 [2048, 1024], P(None, 'tensor'), may hold values from -0.125 to 0.125
- query_gain: bfloat16 [128], replicated, may hold values from 0.5 to 1.5
- key_gain: bfloat16 [128], replicated, may hold values from 0.5 to 1.5
- output_weight: bfloat16 [2048, 2048], P('tensor'), may hold values from -0.75 to 0.75
- feed_gain: bfloat16 [2048], replicated, may hold values from 0.3 to 5, as said below
- gate_weight: bfloat16 [2048, 6144], P(None, 'tensor'), may hold values from -0.125 to 0.125
- up_weight: bfloat16 [2048, 6144], P(None, 'tensor'), may hold values from -0.125 to 0.125
- down_weight: bfloat16 [6144, 2048], P('tensor'), may hold values from -0.078125 to 0.078125
Outputs:
- outputs: bfloat16 [2048, 2048], P(('dp', 'ctx'), 'tensor')
- grad_inputs: float32 [2048, 2048], P(('dp', 'ctx'), 'tensor')
- grad_attention_gain: float32 [2048], P('tensor')
- grad_query_weight: float32 [2048, 2048], P(None, 'tensor')
- grad_key_weight: float32 [2048, 1024], P(None, 'tensor')
- grad_value_weight: float32 [2048, 1024], P(None, 'tensor')
- grad_query_gain: float32 [128], replicated
- grad_key_gain: float32 [128], replicated
- grad_output_weight: float32 [2048, 2048], P('tensor')
- grad_feed_gain: float32 [2048], P('tensor')
- grad_gate_weight: float32 [2048, 6144], P(None, 'tensor')
- grad_up_weight: float32 [2048, 6144], P(None, 'tensor')
- grad_down_weight: float32 [6144, 2048], P('tensor')
Inputs may be any that keep to these rules, and one draw needn't show every extreme that they name: `segments`: in each sequence the document numbers start at 0, never fall, and each document is one run of equal numbers; a sequence holds at most 16 documents. `positions`: a token's position counts from 0 at the first token of its document. `feed_gain`: positive gains.
All inputs are finite; a program needn't handle non-finite values.
Results may differ from a plain program's by a relative error of at most 0.024.
Values may be sent and summed in bfloat16 or wider, within the bound.
No kernel may reach another device: no remote copies, remote signals or barrier semaphores. Data moves between devices by JAX's collectives and lax.ppermute only.
A program may use at most 256 MiB of HBM per device.

v0:
```python
import jax
import jax.numpy as jnp
from jax import lax
from jax.sharding import PartitionSpec as P

HD = 128
EPS = 1e-06
THETA = 1000000.0
NEG = -1e30


def rope_tables(position_row):
    half = HD // 2
    freqs = jnp.exp(-(2.0 * jnp.arange(half, dtype=jnp.float32) / HD) * jnp.log(jnp.float32(THETA)))
    angles = position_row.astype(jnp.float32)[:, None] * freqs[None, :]
    return (jnp.cos(angles)[:, None, :], jnp.sin(angles)[:, None, :])


def rotate(value, cosine, sine):
    half = value.shape[-1] // 2
    first = value[..., :half]
    second = value[..., half:]
    return jnp.concatenate(
        [first * cosine - second * sine, second * cosine + first * sine], axis=-1
    )


def head_prepare(raw, gain, cosine, sine):
    count = raw.shape[0]
    heads = raw.reshape(count, -1, HD)
    normed = heads * lax.rsqrt(jnp.mean(heads * heads, axis=-1, keepdims=True) + EPS) * gain
    return rotate(normed, cosine, sine).reshape(count, -1)


def matmul(left, right):
    return jnp.dot(left, right, preferred_element_type=jnp.float32)


def per_device(
    inputs,
    cotangent,
    segments,
    positions,
    attention_gain,
    query_weight,
    key_weight,
    value_weight,
    query_gain,
    key_gain,
    output_weight,
    feed_gain,
    gate_weight,
    up_weight,
    down_weight,
):
    count = inputs.shape[0]
    shard = inputs.shape[1]
    width = cotangent.shape[1]
    column = lax.axis_index("tensor") * shard
    place = lax.axis_index("ctx")
    kv_local = key_weight.shape[1] // HD
    group = query_weight.shape[1] // key_weight.shape[1]
    factor = HD ** (-0.5)
    block = min(512, count)
    blocks = count // block
    gain_one = attention_gain.astype(jnp.float32)
    gain_two = feed_gain.astype(jnp.float32)
    gain_one_part = lax.dynamic_slice_in_dim(gain_one, column, shard)
    gain_two_part = lax.dynamic_slice_in_dim(gain_two, column, shard)
    cosine, sine = rope_tables(positions[0])
    gathered = lax.all_gather(inputs, "tensor", axis=1, tiled=True).astype(jnp.float32)
    inverse_one = lax.rsqrt(jnp.mean(gathered * gathered, axis=-1, keepdims=True) + EPS)
    unit_one = gathered * inverse_one
    normed_one = (unit_one * gain_one).astype(jnp.bfloat16)
    query_raw = matmul(normed_one, query_weight)
    key_raw = matmul(normed_one, key_weight)
    value_rows = matmul(normed_one, value_weight).astype(jnp.bfloat16)
    query_float, query_pull = jax.vjp(
        lambda raw, gain: head_prepare(raw, gain, cosine, sine),
        query_raw,
        query_gain.astype(jnp.float32),
    )
    key_float, key_pull = jax.vjp(
        lambda raw, gain: head_prepare(raw, gain, cosine, sine),
        key_raw,
        key_gain.astype(jnp.float32),
    )
    query_rows = query_float.astype(jnp.bfloat16)
    key_rows = key_float.astype(jnp.bfloat16)
    segment_row = segments[0]
    all_keys, all_values = (
        lax.all_gather(key_rows, "ctx", axis=0, tiled=True),
        lax.all_gather(value_rows, "ctx", axis=0, tiled=True),
    )
    total_keys = all_keys.shape[0]
    key_index = jnp.arange(total_keys, dtype=jnp.int32)
    row_offset = place * count
    key_heads = all_keys.reshape(total_keys, kv_local, HD)
    value_heads = all_values.reshape(total_keys, kv_local, HD)
    query_blocks = query_rows.reshape(blocks, block, kv_local, group, HD)

    def allowed_mask(index):
        start = index * block
        row_index = row_offset + start + jnp.arange(block, dtype=jnp.int32)
        row_segment = lax.dynamic_slice_in_dim(segment_row, row_offset + start, block)
        return (row_segment[:, None] == segment_row[None, :]) & (
            key_index[None, :] <= row_index[:, None]
        )

    def block_scores(rows, index):
        scores = (
            jnp.einsum("qhgd,khd->hgqk", rows, key_heads, preferred_element_type=jnp.float32)
            * factor
        )
        return jnp.where(allowed_mask(index)[None, None], scores, NEG)

    def forward_block(index):
        rows = query_blocks[index]
        scores = block_scores(rows, index)
        top = jnp.max(scores, axis=-1, keepdims=True)
        raised = jnp.exp(scores - top)
        total = jnp.sum(raised, axis=-1, keepdims=True)
        weights = (raised / total).astype(jnp.bfloat16)
        mixed = jnp.einsum(
            "hgqk,khd->qhgd", weights, value_heads, preferred_element_type=jnp.float32
        )
        return (mixed.astype(jnp.bfloat16), top + jnp.log(total))

    mixed_blocks, log_totals = lax.map(forward_block, jnp.arange(blocks, dtype=jnp.int32))
    mixed_rows = mixed_blocks.reshape(count, -1)
    attention_terms = matmul(mixed_rows, output_weight)
    branch = lax.psum_scatter(attention_terms, "tensor", scatter_dimension=1, tiled=True)
    resid_part = (inputs.astype(jnp.float32) + branch).astype(jnp.bfloat16)
    resid_rows = lax.all_gather(resid_part, "tensor", axis=1, tiled=True).astype(jnp.float32)
    inverse_two = lax.rsqrt(jnp.mean(resid_rows * resid_rows, axis=-1, keepdims=True) + EPS)
    unit_two = resid_rows * inverse_two
    normed_two = (unit_two * gain_two).astype(jnp.bfloat16)
    gate = matmul(normed_two, gate_weight)
    up_rows = matmul(normed_two, up_weight)
    sigmoid = jax.nn.sigmoid(gate)
    silu = gate * sigmoid
    hidden = (silu * up_rows).astype(jnp.bfloat16)
    feed = lax.psum_scatter(
        matmul(hidden, down_weight).astype(jnp.bfloat16), "tensor", scatter_dimension=1, tiled=True
    ).astype(jnp.float32)
    outputs = (resid_part.astype(jnp.float32) + feed).astype(jnp.bfloat16)
    grad_down = matmul(hidden.T, cotangent)
    grad_hidden = matmul(cotangent, down_weight.T)
    grad_gate = (grad_hidden * up_rows * sigmoid * (1.0 + gate * (1.0 - sigmoid))).astype(
        jnp.bfloat16
    )
    grad_up = (grad_hidden * silu).astype(jnp.bfloat16)
    grad_gate_w = matmul(normed_two.T, grad_gate)
    grad_up_w = matmul(normed_two.T, grad_up)
    grad_normed_two = matmul(grad_gate, gate_weight.T) + matmul(grad_up, up_weight.T)
    unit_two_part = lax.dynamic_slice_in_dim(unit_two, column, shard, 1)
    grad_out_part = lax.dynamic_slice_in_dim(cotangent, column, shard, 1).astype(jnp.float32)
    grad_two_part = lax.psum_scatter(grad_normed_two, "tensor", scatter_dimension=1, tiled=True)
    row_term_two = jnp.sum(gain_two_part * grad_two_part * unit_two_part, axis=-1)
    row_total_two = lax.psum(row_term_two, "tensor")
    grad_feed_gain = jnp.sum(grad_two_part * unit_two_part, axis=0)
    grad_resid = (
        grad_out_part
        + inverse_two * (gain_two_part * grad_two_part)
        - unit_two_part * (inverse_two / width) * row_total_two[:, None]
    )
    grad_resid_rows = lax.all_gather(grad_resid.astype(jnp.bfloat16), "tensor", axis=1, tiled=True)
    grad_output_w = matmul(mixed_rows.T, grad_resid_rows)
    grad_mixed = matmul(grad_resid_rows, output_weight.T).astype(jnp.bfloat16)
    grad_mixed_blocks = grad_mixed.reshape(blocks, block, kv_local, group, HD)

    def backward_block(carry, index):
        key_total, value_total = carry
        rows = query_blocks[index]
        grad_rows = grad_mixed_blocks[index]
        scores = block_scores(rows, index)
        probs = jnp.exp(scores - log_totals[index])
        grad_probs = jnp.einsum(
            "qhgd,khd->hgqk", grad_rows, value_heads, preferred_element_type=jnp.float32
        )
        delta = jnp.sum(probs * grad_probs, axis=-1, keepdims=True)
        grad_scores = (probs * (grad_probs - delta)).astype(jnp.bfloat16)
        grad_query = (
            jnp.einsum("hgqk,khd->qhgd", grad_scores, key_heads, preferred_element_type=jnp.float32)
            * factor
        )
        key_total = (
            key_total
            + jnp.einsum("hgqk,qhgd->khd", grad_scores, rows, preferred_element_type=jnp.float32)
            * factor
        )
        value_total = value_total + jnp.einsum(
            "hgqk,qhgd->khd",
            probs.astype(jnp.bfloat16),
            grad_rows,
            preferred_element_type=jnp.float32,
        )
        return ((key_total, value_total), grad_query)

    empty = jnp.zeros((total_keys, kv_local, HD), jnp.float32)
    (key_total, value_total), grad_query_blocks = lax.scan(
        backward_block, (empty, empty), jnp.arange(blocks, dtype=jnp.int32)
    )
    grad_query_rows = grad_query_blocks.reshape(count, -1)
    key_total = key_total.reshape(total_keys, -1)
    value_total = value_total.reshape(total_keys, -1)
    grad_key_rot, grad_value = (
        lax.psum_scatter(
            key_total.astype(jnp.bfloat16), "ctx", scatter_dimension=0, tiled=True
        ).astype(jnp.float32),
        lax.psum_scatter(
            value_total.astype(jnp.bfloat16), "ctx", scatter_dimension=0, tiled=True
        ).astype(jnp.float32),
    )
    grad_query_raw, grad_query_gain = query_pull(grad_query_rows)
    grad_key_raw, grad_key_gain = key_pull(grad_key_rot)
    grad_query_low = grad_query_raw.astype(jnp.bfloat16)
    grad_key_low = grad_key_raw.astype(jnp.bfloat16)
    grad_value_low = grad_value.astype(jnp.bfloat16)
    grad_query_w = matmul(normed_one.T, grad_query_low)
    grad_key_w = matmul(normed_one.T, grad_key_low)
    grad_value_w = matmul(normed_one.T, grad_value_low)
    grad_normed_one = (
        matmul(grad_query_low, query_weight.T)
        + matmul(grad_key_low, key_weight.T)
        + matmul(grad_value_low, value_weight.T)
    )
    grad_one_part = lax.psum_scatter(
        grad_normed_one.astype(jnp.bfloat16), "tensor", scatter_dimension=1, tiled=True
    ).astype(jnp.float32)
    unit_one_part = lax.dynamic_slice_in_dim(unit_one, column, shard, 1)
    row_term_one = jnp.sum(gain_one_part * grad_one_part * unit_one_part, axis=-1)
    row_total_one, query_gain_total, key_gain_total = lax.psum(
        (row_term_one, grad_query_gain, grad_key_gain), "tensor"
    )
    grad_inputs = (
        grad_resid
        + inverse_one * (gain_one_part * grad_one_part)
        - unit_one_part * (inverse_one / width) * row_total_one[:, None]
    )
    grad_attention_gain = jnp.sum(grad_one_part * unit_one_part, axis=0)
    summed = (
        lax.psum(grad_attention_gain.astype(jnp.bfloat16), ("dp", "ctx")).astype(jnp.float32),
        lax.psum(grad_query_w.astype(jnp.bfloat16), ("dp", "ctx")).astype(jnp.float32),
        lax.psum(grad_key_w.astype(jnp.bfloat16), ("dp", "ctx")).astype(jnp.float32),
        lax.psum(grad_value_w.astype(jnp.bfloat16), ("dp", "ctx")).astype(jnp.float32),
        lax.psum(query_gain_total.astype(jnp.bfloat16), ("dp", "ctx")).astype(jnp.float32),
        lax.psum(key_gain_total.astype(jnp.bfloat16), ("dp", "ctx")).astype(jnp.float32),
        lax.psum(grad_output_w.astype(jnp.bfloat16), ("dp", "ctx")).astype(jnp.float32),
        lax.psum(grad_feed_gain.astype(jnp.bfloat16), ("dp", "ctx")).astype(jnp.float32),
        lax.psum(grad_gate_w.astype(jnp.bfloat16), ("dp", "ctx")).astype(jnp.float32),
        lax.psum(grad_up_w.astype(jnp.bfloat16), ("dp", "ctx")).astype(jnp.float32),
        lax.psum(grad_down.astype(jnp.bfloat16), ("dp", "ctx")).astype(jnp.float32),
    )
    return (outputs, grad_inputs) + tuple(summed)


def solution(mesh):
    in_specs = (
        P(("dp", "ctx"), "tensor"),
        P(("dp", "ctx"), None),
        P("dp", None),
        P("dp", "ctx"),
        P(),
        P(None, "tensor"),
        P(None, "tensor"),
        P(None, "tensor"),
        P(),
        P(),
        P("tensor", None),
        P(),
        P(None, "tensor"),
        P(None, "tensor"),
        P("tensor", None),
    )
    out_specs = (
        P(("dp", "ctx"), "tensor"),
        P(("dp", "ctx"), "tensor"),
        P("tensor"),
        P(None, "tensor"),
        P(None, "tensor"),
        P(None, "tensor"),
        P(),
        P(),
        P("tensor", None),
        P("tensor"),
        P(None, "tensor"),
        P(None, "tensor"),
        P("tensor", None),
    )
    return jax.shard_map(
        per_device, mesh=mesh, in_specs=in_specs, out_specs=out_specs, check_vma=False
    )
```

profile of v0, /device:TPU:0, one launch (start us, length us, event | category | flops | bytes accessed | tf_op | source)
XLA Modules:
  0.0 697.9 jit_solution(3110859281240040887)
XLA Ops:
  15.3 24.9 %all-gather.4.cloned.1.call-done = bf16[256,2048]{1,0:T(8,128)(2,1)} async-done(((bf16[256,512]{1,0:T(8,128)(2,1)}), bf16[256,2048]{1,0:T(8,128)(2,1)}) %all-gather.4.cloned.1.call-update) | async-done | bytes 1048592 | tf_op jit(solution)/shard_map/all_gather | solution.py:71
  42.3 2.0 convolution_convert_fusion.10
  44.4 5.8 all_gather.16
  50.9 2.0 multiply_reduce_fusion.7
  54.4 5.8 all_gather.17
  60.2 1.6 fusion.35
  68.2 2.0 fusion.40
  70.3 43.7 %reduce-scatter.7.cloned.1.call-done = f32[256,512]{1,0:T(8,128)} async-done(((f32[256,2048]{1,0:T(8,128)}), f32[256,512]{1,0:T(8,128)}) %reduce-scatter.7.cloned.1.call-update) | async-done | bytes 524304 | tf_op jit(solution)/shard_map/reduce_scatter | solution.py:132
  114.1 1.8 add_convert_fusion.1
  116.3 27.0 %all-gather.6.cloned.1.call-done = bf16[256,2048]{1,0:T(8,128)(2,1)} async-done(((bf16[256,512]{1,0:T(8,128)(2,1)}), bf16[256,2048]{1,0:T(8,128)(2,1)}) %all-gather.6.cloned.1.call-update) | async-done | bytes 1048592 | tf_op jit(solution)/shard_map/all_gather | solution.py:134
  143.3 1.7 fusion.3
  145.6 5.8 fusion.33
  151.4 1.9 fusion.34
  153.4 3.3 multiply_convert_fusion.2
  156.7 1.8 fusion.41
  158.6 3.2 convolution_add_fusion.1
  164.1 41.2 %reduce-scatter.11.cloned.1.call-done = f32[256,512]{1,0:T(8,128)} async-done(((f32[256,2048]{1,0:T(8,128)}), f32[256,512]{1,0:T(8,128)}) %reduce-scatter.11.cloned.1.call-update) | async-done | bytes 524304 | tf_op jit(solution)/shard_map/reduce_scatter | solution.py:158
  205.3 2.0 multiply_reduce_fusion
  207.2 10.5 %psum.105 = f32[256]{0:T(256)} all-reduce(f32[256]{0:T(256)} %get-tuple-element.70), channel_id=1, replica_groups=mesh['dp'=4,'ctx'=2,'tensor'=4] {'tensor'}, use_global_device_ids=true, to_apply=%region_10.11 | all-reduce | flops 256 | bytes 2048 | tf_op jit(solution)/shard_map/psum | solution.py:160
  217.8 2.4 fusion.37
  220.9 25.7 %all-gather.8.cloned.1.call-done = bf16[256,2048]{1,0:T(8,128)(2,1)} async-done(((bf16[256,512]{1,0:T(8,128)(2,1)}), bf16[256,2048]{1,0:T(8,128)(2,1)}) %all-gather.8.cloned.1.call-update) | async-done | bytes 1048592 | tf_op jit(solution)/shard_map/all_gather | solution.py:167
  246.6 2.7 convolution_convert_fusion.8
  249.2 1.8 copy.115
  251.0 2.4 fusion.4
  256.2 2.2 fusion.12
  258.4 10.1 %reduce-scatter.9.cloned.1.call-start = ((), (), s32[]{:S(2)}) async-start(), calls=%async_computation.9 | async-start | bytes 1310720 | tf_op jit(solution)/shard_map/reduce_scatter | solution.py:143
  268.5 5.9 convolution_convert_fusion.7
  278.4 2.2 multiply_reduce_fusion.1
  280.9 1.6 fusion.21
  285.0 1.9 fusion.43
  287.0 1.8 fusion.1
  288.9 6.1 convolution_convert_fusion
  294.9 4.7 convolution_convert_fusion.1
  299.6 4.7 convolution_convert_fusion.2
  304.3 2.0 convolution_convert_fusion.3
  306.3 2.2 convolution_convert_fusion.4
  308.5 1.6 convolution_convert_fusion.5
  313.3 1.7 add_convert_fusion
  315.0 25.9 %reduce-scatter.17.cloned.1.call-done = bf16[256,512]{1,0:T(8,128)(2,1)} async-done(((bf16[256,2048]{1,0:T(8,128)(2,1)}), bf16[256,512]{1,0:T(8,128)(2,1)}) %reduce-scatter.17.cloned.1.call-update) | async-done | bytes 262160 | tf_op jit(solution)/shard_map/reduce_scatter | solution.py:228
  342.1 9.7 %all-reduce.4 = (f32[256]{0:T(256)S(1)}, bf16[128]{0:T(256)(128)(2,1)S(1)}, bf16[128]{0:T(256)(128)(2,1)S(1)}) all-reduce(f32[256]{0:T(256)S(1)} %get-tuple-element.72, f32[128]{0:T(128)S(1)} %copy-done.63, f32[128]{0:T(128)S(1)} %copy-done.64), channel_id=1, replica_groups=mesh['dp'=4,'ctx'=2,'tensor'=4] {'tensor'}, use_global_device_ids=true, to_apply=%region_18.19 | all-reduce | flops 512 | bytes 3584 | tf_op jit(solution)/shard_map/psum | solution.py:233
  351.8 14.3 %all-reduce.5 = (bf16[512]{0:T(512)(128)(2,1)S(1)}, bf16[128]{0:T(256)(128)(2,1)S(1)}, bf16[128]{0:T(256)(128)(2,1)S(1)}, bf16[512]{0:T(512)(128)(2,1)S(1)}) all-reduce(bf16[512]{0:T(512)(128)(2,1)S(1)} %get-tuple-element.71, bf16[128]{0:T(256)(128)(2,1)S(1)} %get-tuple-element.78, ...), channel_id=1, replica_groups=mesh['dp'=4,'ctx'=2,'tensor'=4] {'dp','ctx'}, use_global_device_ids=true, to_apply=%region_20.21 | all-reduce | flops 1280 | bytes 5120 | tf_op jit(solution)/shard_map/psum | solution.py:243
  368.3 2.1 fusion.18
  370.4 287.2 %all-reduce.9.cloned.1.call-done = (bf16[2048,512]{1,0:T(8,128)(2,1)}, bf16[2048,256]{1,0:T(8,128)(2,1)}, bf16[2048,256]{1,0:T(8,128)(2,1)}, bf16[512,2048]{1,0:...) async-done(((bf16[2048,512]{1,0:T(8,128)(2,1)}, bf16[2048,256]{1,0:T(8,128)(2,1)}, bf16[2048,256]{1,0:T(8,128)(2,1)}, ...) | async-done | bytes 25165840 | tf_op jit(solution)/shard_map/psum | solution.py:244
  657.6 4.3 convert_element_type.251
  665.8 2.7 convert_element_type.261
  668.4 9.5 %convert_element_type.265 = f32[2048,1536]{1,0:T(8,128)} convert(bf16[2048,1536]{1,0:T(8,128)(2,1)} %get-tuple-element.101) | non-fusion elementwise | flops 3145728 | bytes 18874368 | tf_op jit(solution)/shard_map/convert_element_type | solution.py:251
  677.9 6.6 convert_element_type.267
  684.5 6.3 convert_element_type.269
  (238 shorter events, 42.7 us)
Async XLA Ops:
  7.2 61.0 %copy-start = (bf16[512,2048]{1,0:T(8,128)(2,1)S(1)}, bf16[512,2048]{1,0:T(8,128)(2,1)}, u32[]{:S(2)}) copy-start(bf16[512,2048]{1,0:T(8,128)(2,1)} %param.25) | copy-start | bytes 6291460
  7.2 33.1 %all-gather.4.cloned.1.call-start = ((), (), s32[]{:S(2)}) async-start(), calls=%async_computation.6 | async-start | bytes 1310720 | tf_op jit(solution)/shard_map/all_gather | solution.py:71
  7.9 106.1 %reduce-scatter.7.cloned.1.call-start = ((), (), s32[]{:S(2)}) async-start(), calls=%async_computation.7 | async-start | bytes 2621440 | tf_op jit(solution)/shard_map/reduce_scatter | solution.py:132
  8.6 55.5 %copy-start.58 = (f32[128]{0:T(128)}, f32[128]{0:T(128)S(1)}, u32[]{:S(2)}) copy-start(f32[128]{0:T(128)S(1)} %convert_element_type.215) | copy-start | bytes 1540
  11.2 49.0 %copy-start.56 = (f32[2048]{0:T(1024)}, f32[2048]{0:T(1024)S(1)}, u32[]{:S(2)}) copy-start(f32[2048]{0:T(1024)S(1)} %convert_element_type.208) | copy-start | bytes 24580
  11.7 28.5 %copy-start.16 = (f32[256,64]{1,0:T(8,128)}, f32[256,64]{1,0:T(8,128)S(1)}, u32[]{:S(2)}) copy-start(f32[256,64]{1,0:T(8,128)S(1)} %get-tuple-element.120) | copy-start | bytes 196612
  41.8 9.1 %copy-start.9 = (bf16[256,2048]{1,0:T(8,128)(2,1)S(1)}, bf16[256,2048]{1,0:T(8,128)(2,1)}, u32[]{:S(2)}) copy-start(bf16[256,2048]{1,0:T(8,128)(2,1)} %all-gather.4.cloned.1.call-done) | copy-start | bytes 3145732
  42.3 17.8 %copy-start.50 = (f32[256]{0:T(256)}, f32[256]{0:T(256)S(1)}, u32[]{:S(2)}) copy-start(f32[256]{0:T(256)S(1)} %get-tuple-element.122) | copy-start | bytes 3076
  50.9 9.3 %copy-start.22 = (bf16[2048,512]{1,0:T(8,128)(2,1)S(1)}, bf16[2048,512]{1,0:T(8,128)(2,1)}, u32[]{:S(2)}) copy-start(bf16[2048,512]{1,0:T(8,128)(2,1)} %param.20) | copy-start | bytes 6291460
  53.0 7.2 %copy-start.54 = (f32[256,2]{0,1:T(2,128)}, f32[256,2]{0,1:T(2,128)S(1)}, u32[]{:S(2)}) copy-start(f32[256,2]{0,1:T(2,128)S(1)} %get-tuple-element.125) | copy-start | bytes 6148
  70.2 43.8 %copy-start.30 = (bf16[256,512]{1,0:T(8,128)(2,1)S(1)}, bf16[256,512]{1,0:T(8,128)(2,1)}, u32[]{:S(2)}) copy-start(bf16[256,512]{1,0:T(8,128)(2,1)} %param.15) | copy-start | bytes 786436
  70.2 46.1 %copy-start.52 = (bf16[2048]{0:T(1024)(128)(2,1)S(1)}, bf16[2048]{0:T(1024)(128)(2,1)}, u32[]{:S(2)}) copy-start(bf16[2048]{0:T(1024)(128)(2,1)} %param.26) | copy-start | bytes 12292
  70.3 73.0 %all-gather.6.cloned.1.call-start = ((), (), s32[]{:S(2)}) async-start(), calls=%async_computation.8 | async-start | bytes 1310720 | tf_op jit(solution)/shard_map/all_gather | solution.py:134
  115.9 89.4 %reduce-scatter.11.cloned.1.call-start = ((), (), s32[]{:S(2)}) async-start(), calls=%async_computation.10 | async-start | bytes 2621440 | tf_op jit(solution)/shard_map/reduce_scatter | solution.py:158
  143.3 8.0 %slice-start.4 = ((s8[6291456]{0:T(1024)(128)(4,1)}), s8[4194304]{0:T(1024)(128)(4,1)S(1)}, s32[]{:S(2)}) async-start(s8[6291456]{0:T(1024)(128)(4,1)} %bitcast.132), calls=%async_computation.20 | async-start | bytes 8388608
  143.3 10.0 %slice-start.8 = ((s8[6291456]{0:T(1024)(128)(4,1)}), s8[4194304]{0:T(1024)(128)(4,1)S(1)}, s32[]{:S(2)}) async-start(s8[6291456]{0:T(1024)(128)(4,1)} %bitcast.136), calls=%async_computation.24 | async-start | bytes 8388608
  145.6 5.8 copy-start.4
  145.6 5.8 slice-start.5
  145.6 7.8 %slice-start.9 = ((s8[6291456]{0:T(1024)(128)(4,1)}), s8[2097152]{0:T(1024)(128)(4,1)S(1)}, s32[]{:S(2)}) async-start(s8[6291456]{0:T(1024)(128)(4,1)} %bitcast.136), calls=%async_computation.25 | async-start | bytes 4194304
  151.4 7.2 %slice-start.6 = ((s8[6291456]{0:T(1024)(128)(4,1)}), s8[4194304]{0:T(1024)(128)(4,1)S(1)}, s32[]{:S(2)}) async-start(s8[6291456]{0:T(1024)(128)(4,1)} %bitcast.134), calls=%async_computation.22 | async-start | bytes 8388608
  153.4 5.2 slice-start.7
  161.8 84.8 %all-gather.8.cloned.1.call-start = ((), (), s32[]{:S(2)}) async-start(), calls=%async_computation.11 | async-start | bytes 1310720 | tf_op jit(solution)/shard_map/all_gather | solution.py:167
  220.1 62.4 %reduce-scatter.13.cloned.1.call-start = ((), (), s32[]{:S(2)}) async-start(), calls=%async_computation.12 | async-start | bytes 393216 | tf_op jit(solution)/shard_map/reduce_scatter | solution.py:208
  256.2 28.8 %reduce-scatter.15.cloned.1.call-start = ((), (), s32[]{:S(2)}) async-start(), calls=%async_computation.13 | async-start | bytes 393216 | tf_op jit(solution)/shard_map/reduce_scatter | solution.py:211
  258.4 54.3 %reduce-scatter.9.cloned.1.call-start = ((), (), s32[]{:S(2)}) async-start(), calls=%async_computation.9 | async-start | bytes 1310720 | tf_op jit(solution)/shard_map/reduce_scatter | solution.py:143
  268.5 6.0 copy-start.8
  268.5 6.0 copy-start.13
  274.4 66.5 %reduce-scatter.17.cloned.1.call-start = ((), (), s32[]{:S(2)}) async-start(), calls=%async_computation.14 | async-start | bytes 1310720 | tf_op jit(solution)/shard_map/reduce_scatter | solution.py:228
  276.9 3.8 copy-start.46
  276.9 4.0 copy-start.59
  278.4 5.1 copy-start.39
  278.4 5.1 copy-start.41
  280.6 3.7 copy-start.55
  288.8 6.1 copy-start.37
  288.8 368.8 %all-reduce.9.cloned.1.call-start = ((), (), s32[]{:S(2)}) async-start(), calls=%async_computation.15 | async-start | bytes 50331648 | tf_op jit(solution)/shard_map/psum | solution.py:244
  294.9 4.7 copy-start.35
  299.6 4.7 copy-start.29
  299.6 4.7 copy-start.32
  312.4 29.6 %copy-start.63 = (f32[128]{0:T(128)S(1)}, f32[128]{0:T(128)}, u32[]{:S(2)}) copy-start(f32[128]{0:T(128)} %get-tuple-element.73) | copy-start | bytes 1540
  312.4 29.6 %copy-start.64 = (f32[128]{0:T(128)S(1)}, f32[128]{0:T(128)}, u32[]{:S(2)}) copy-start(f32[128]{0:T(128)} %get-tuple-element.75) | copy-start | bytes 1540
  312.4 39.4 %copy-start.62 = (bf16[512]{0:T(512)(128)(2,1)S(1)}, bf16[512]{0:T(512)(128)(2,1)}, u32[]{:S(2)}) copy-start(bf16[512]{0:T(512)(128)(2,1)} %get-tuple-element.69) | copy-start | bytes 3076
  312.4 55.9 %copy-start.61 = (f32[256]{0:T(256)S(1)}, f32[256]{0:T(256)}, u32[]{:S(2)}) copy-start(f32[256]{0:T(256)} %get-tuple-element.121) | copy-start | bytes 3076
  657.6 4.3 copy-start.27
  665.8 12.2 %slice-start.2 = ((s8[6291456]{0:T(1024)(128)(4,1)}), s8[4194304]{0:T(1024)(128)(4,1)S(1)}, s32[]{:S(2)}) async-start(s8[6291456]{0:T(1024)(128)(4,1)} %bitcast.107), calls=%async_computation.18 | async-start | bytes 8388608
  668.4 9.5 %slice-start.3 = ((s8[6291456]{0:T(1024)(128)(4,1)}), s8[2097152]{0:T(1024)(128)(4,1)S(1)}, s32[]{:S(2)}) async-start(s8[6291456]{0:T(1024)(128)(4,1)} %bitcast.107), calls=%async_computation.19 | async-start | bytes 4194304
  668.4 16.1 %slice-start = ((s8[6291456]{0:T(1024)(128)(4,1)}), s8[4194304]{0:T(1024)(128)(4,1)S(1)}, s32[]{:S(2)}) async-start(s8[6291456]{0:T(1024)(128)(4,1)} %bitcast.105), calls=%async_computation.16 | async-start | bytes 8388608
  677.9 6.6 slice-start.1
  684.5 6.3 copy-start.1
  (37 other events, 69.0 us)
Sparse Core Ops, SparseCore 0:
  9.6 30.6 all-gather.3
  70.4 43.6 reduce-scatter.6
  116.0 27.2 all-gather.5
  161.9 43.3 reduce-scatter.10
  220.3 26.2 all-gather.7
  256.3 11.1 reduce-scatter.12
  270.3 11.6 reduce-scatter.14
  284.9 27.1 reduce-scatter.8
  315.1 25.7 reduce-scatter.16
  346.9 310.6 all-reduce.8
where the time goes:
time: 704 us; the launch traced here: 698 us
  waiting for transfers between devices  476 us (68%)
  other arithmetic  67.8 us (10%)
  matrix products  66.3 us (9%)
  blocking collectives  46.1 us (7%)
  between operations  15.3 us (2%)
  local copies, waits for them, and re-layouts  15.1 us (2%)
  starting transfers between devices  10.8 us (2%)
    psum x1, waiting for transfers between devices, per_device(): lax.psum(grad_query_w.astype(jnp.bfloat16), ('dp', 'ctx'))  287 us
    dot_general x21, matrix products, matmul(): return jnp.dot(left, right, preferred_element_type=jnp.float32)  59.2 us
    reduce_scatter x1, waiting for transfers between devices, per_device(): lax.psum_scatter(attention_terms, 'tensor', scatter_dimension=1, tiled=True)  43.7 us
    reduce_scatter x1, waiting for transfers between devices, per_device(): lax.psum_scatter(grad_normed_two, 'tensor', scatter_dimension=1, tiled=True)  41.2 us
    all_gather x1, waiting for transfers between devices, per_device(): lax.all_gather(resid_part, 'tensor', axis=1, tiled=True).astype(jnp.float32)  27 us
    reduce_scatter x1, waiting for transfers between devices, per_device(): lax.psum_scatter(grad_normed_one.astype(jnp.bfloat16), 'tensor', scatter_...  25.9 us
    all_gather x1, waiting for transfers between devices, per_device(): lax.all_gather(grad_resid.astype(jnp.bfloat16), 'tensor', axis=1, tiled=T...  25.7 us
    all_gather x1, waiting for transfers between devices, per_device(): lax.all_gather(inputs, 'tensor', axis=1, tiled=True).astype(jnp.float32)  24.9 us
  transfers between devices with their start and end apart: 10, of which 7 were waited for; matrix products, arithmetic and copies ran while one was open for 9% of the time, Pallas kernels for 0%

commit v1 on v0

--- a/solution.py
+++ b/solution.py
@@ -241,7 +241,9 @@
     grad_attention_gain = jnp.sum(grad_one_part * unit_one_part, axis=0)
     summed = (
         lax.psum(grad_attention_gain.astype(jnp.bfloat16), ("dp", "ctx")).astype(jnp.float32),
-        lax.psum(grad_query_w.astype(jnp.bfloat16), ("dp", "ctx")).astype(jnp.float32),
+        jnp.sum(lax.all_gather(grad_query_w.astype(jnp.bfloat16), ("dp", "ctx")), axis=0).astype(
+            jnp.float32
+        ),
         lax.psum(grad_key_w.astype(jnp.bfloat16), ("dp", "ctx")).astype(jnp.float32),
         lax.psum(grad_value_w.astype(jnp.bfloat16), ("dp", "ctx")).astype(jnp.float32),
         lax.psum(query_gain_total.astype(jnp.bfloat16), ("dp", "ctx")).astype(jnp.float32),

time: 704 us -> 755 us (1.072)
  waiting for transfers between devices: 476 us -> 516 us
  other arithmetic: 67.8 us -> 80.8 us
    all_gather x0 -> x1, waiting for transfers between devices: none -> 61.3 us  [per_device(): lax.all_gather(grad_query_w.astype(jnp.bfloat16), ('dp', 'ctx'))]
    psum x1, waiting for transfers between devices: 287 us -> 264 us  [per_device(): lax.psum(grad_key_w.astype(jnp.bfloat16), ('dp', 'ctx')).astype(jnp.float32)]
    reduce_sum x0 -> x1, other arithmetic: none -> 10.7 us  [per_device(): jnp.sum(lax.all_gather(grad_query_w.astype(jnp.bfloat16), ('dp', 'ctx')),...]
  transfers between devices with their start and end apart: 10 -> 11, of which waited for: 7 -> 8; matrix products, arithmetic and copies ran while one was open for 9% -> 12% of each run, Pallas kernels for 0% -> 0%
where the time goes in v1:
time: 755 us; the launch traced here: 748 us
  waiting for transfers between devices  516 us (68%)
  other arithmetic  80.8 us (11%)
  matrix products  65.6 us (9%)
  blocking collectives  46 us (6%)
  between operations  15 us (2%)
  local copies, waits for them, and re-layouts  14.4 us (2%)
  starting transfers between devices  10.9 us (1%)
    psum x1, waiting for transfers between devices, per_device(): lax.psum(grad_key_w.astype(jnp.bfloat16), ('dp', 'ctx')).astype(jnp.float32)  264 us
    all_gather x1, waiting for transfers between devices, per_device(): lax.all_gather(grad_query_w.astype(jnp.bfloat16), ('dp', 'ctx'))  61.3 us
    dot_general x21, matrix products, matmul(): return jnp.dot(left, right, preferred_element_type=jnp.float32)  58.5 us
    reduce_scatter x1, waiting for transfers between devices, per_device(): lax.psum_scatter(attention_terms, 'tensor', scatter_dimension=1, tiled=True)  43.8 us
    reduce_scatter x1, waiting for transfers between devices, per_device(): lax.psum_scatter(grad_normed_two, 'tensor', scatter_dimension=1, tiled=True)  41.2 us
    all_gather x1, waiting for transfers between devices, per_device(): lax.all_gather(resid_part, 'tensor', axis=1, tiled=True).astype(jnp.float32)  27 us
    reduce_scatter x1, waiting for transfers between devices, per_device(): lax.psum_scatter(grad_normed_one.astype(jnp.bfloat16), 'tensor', scatter_...  26.4 us
    all_gather x1, waiting for transfers between devices, per_device(): lax.all_gather(grad_resid.astype(jnp.bfloat16), 'tensor', axis=1, tiled=T...  25.6 us
  transfers between devices with their start and end apart: 11, of which 8 were waited for; matrix products, arithmetic and copies ran while one was open for 12% of the time, Pallas kernels for 0%

profile of v1, /device:TPU:0, one launch (start us, length us, event | category | flops | bytes accessed | tf_op | source)
XLA Modules:
  0.0 748.2 jit_solution(1584125095717306505)
XLA Ops:
  15.3 24.9 %all-gather.6.cloned.1.call-done = bf16[256,2048]{1,0:T(8,128)(2,1)} async-done(((bf16[256,512]{1,0:T(8,128)(2,1)}), bf16[256,2048]{1,0:T(8,128)(2,1)}) %all-gather.6.cloned.1.call-update) | async-done | bytes 1048592 | tf_op jit(solution)/shard_map/all_gather | solution.py:71
  42.3 2.0 convolution_convert_fusion.10
  44.4 5.8 all_gather.22
  50.9 2.0 multiply_reduce_fusion.7
  54.4 5.8 all_gather.23
  68.2 2.0 fusion.40
  70.3 43.8 %reduce-scatter.7.cloned.1.call-done = f32[256,512]{1,0:T(8,128)} async-done(((f32[256,2048]{1,0:T(8,128)}), f32[256,512]{1,0:T(8,128)}) %reduce-scatter.7.cloned.1.call-update) | async-done | bytes 524304 | tf_op jit(solution)/shard_map/reduce_scatter | solution.py:132
  114.1 1.8 add_convert_fusion.1
  116.4 27.0 %all-gather.8.cloned.1.call-done = bf16[256,2048]{1,0:T(8,128)(2,1)} async-done(((bf16[256,512]{1,0:T(8,128)(2,1)}), bf16[256,2048]{1,0:T(8,128)(2,1)}) %all-gather.8.cloned.1.call-update) | async-done | bytes 1048592 | tf_op jit(solution)/shard_map/all_gather | solution.py:134
  143.4 1.7 fusion.3
  145.6 5.1 fusion.33
  150.8 1.9 fusion.34
  152.7 3.3 multiply_convert_fusion.2
  156.1 1.8 fusion.41
  157.9 3.2 convolution_add_fusion.1
  163.4 41.2 %reduce-scatter.11.cloned.1.call-done = f32[256,512]{1,0:T(8,128)} async-done(((f32[256,2048]{1,0:T(8,128)}), f32[256,512]{1,0:T(8,128)}) %reduce-scatter.11.cloned.1.call-update) | async-done | bytes 524304 | tf_op jit(solution)/shard_map/reduce_scatter | solution.py:158
  204.6 2.0 multiply_reduce_fusion
  206.6 10.5 %psum.98 = f32[256]{0:T(256)} all-reduce(f32[256]{0:T(256)} %get-tuple-element.70), channel_id=1, replica_groups=mesh['dp'=4,'ctx'=2,'tensor'=4] {'tensor'}, use_global_device_ids=true, to_apply=%region_10.11 | all-reduce | flops 256 | bytes 2048 | tf_op jit(solution)/shard_map/psum | solution.py:160
  217.1 2.4 fusion.37
  220.3 25.6 %all-gather.10.cloned.1.call-done = bf16[256,2048]{1,0:T(8,128)(2,1)} async-done(((bf16[256,512]{1,0:T(8,128)(2,1)}), bf16[256,2048]{1,0:T(8,128)(2,1)}) %all-gather.10.cloned.1.call-update) | async-done | bytes 1048592 | tf_op jit(solution)/shard_map/all_gather | solution.py:167
  245.9 2.7 convolution_convert_fusion.8
  248.6 1.8 copy.115
  250.4 2.4 fusion.4
  255.6 2.2 fusion.12
  257.8 10.1 %reduce-scatter.9.cloned.1.call-start = ((), (), s32[]{:S(2)}) async-start(), calls=%async_computation.9 | async-start | bytes 1310720 | tf_op jit(solution)/shard_map/reduce_scatter | solution.py:143
  267.9 5.9 convolution_convert_fusion.7
  277.8 2.2 multiply_reduce_fusion.1
  284.4 1.9 fusion.43
  286.4 1.8 fusion.1
  288.3 6.1 convolution_convert_fusion
  294.3 4.7 convolution_convert_fusion.1
  299.0 4.6 convolution_convert_fusion.2
  303.7 2.0 convolution_convert_fusion.3
  309.0 2.2 convolution_convert_fusion.4
  312.1 1.7 add_convert_fusion
  313.9 26.4 %reduce-scatter.17.cloned.1.call-done = bf16[256,512]{1,0:T(8,128)(2,1)} async-done(((bf16[256,2048]{1,0:T(8,128)(2,1)}), bf16[256,512]{1,0:T(8,128)(2,1)}) %reduce-scatter.17.cloned.1.call-update) | async-done | bytes 262160 | tf_op jit(solution)/shard_map/reduce_scatter | solution.py:228
  341.4 9.7 %all-reduce.4 = (f32[256]{0:T(256)S(1)}, bf16[128]{0:T(256)(128)(2,1)S(1)}, bf16[128]{0:T(256)(128)(2,1)S(1)}) all-reduce(f32[256]{0:T(256)S(1)} %get-tuple-element.72, f32[128]{0:T(128)S(1)} %copy-done.62, f32[128]{0:T(128)S(1)} %copy-done.63), channel_id=1, replica_groups=mesh['dp'=4,'ctx'=2,'tensor'=4] {'tensor'}, use_global_device_ids=true, to_apply=%region_18.19 | all-reduce | flops 512 | bytes 3584 | tf_op jit(solution)/shard_map/psum | solution.py:233
  351.1 14.2 %all-reduce.5 = (bf16[512]{0:T(512)(128)(2,1)S(1)}, bf16[128]{0:T(256)(128)(2,1)S(1)}, bf16[128]{0:T(256)(128)(2,1)S(1)}, bf16[512]{0:T(512)(128)(2,1)S(1)}) all-reduce(bf16[512]{0:T(512)(128)(2,1)S(1)} %get-tuple-element.71, bf16[128]{0:T(256)(128)(2,1)S(1)} %get-tuple-element.78, ...), channel_id=1, replica_groups=mesh['dp'=4,'ctx'=2,'tensor'=4] {'dp','ctx'}, use_global_device_ids=true, to_apply=%region_20.21 | all-reduce | flops 1280 | bytes 5120 | tf_op jit(solution)/shard_map/psum | solution.py:243
  367.5 2.1 fusion.18
  369.7 264.4 %all-reduce.9.cloned.1.call-done = (bf16[2048,256]{1,0:T(8,128)(2,1)}, bf16[2048,256]{1,0:T(8,128)(2,1)}, bf16[512,2048]{1,0:T(8,128)(2,1)}, bf16[2048,1536]{1,0...) async-done(((bf16[2048,256]{1,0:T(8,128)(2,1)}, bf16[2048,256]{1,0:T(8,128)(2,1)}, bf16[512,2048]{1,0:T(8,128)(2,1)}, bf16[2048,1536]{1,0:T(8,128)(2,1)}, ...) | async-done | bytes 23068688 | tf_op jit(solution)/shard_map/psum | solution.py:247
  634.1 2.8 convert_element_type.255
  639.2 2.7 convert_element_type.263
  641.9 10.5 %convert_element_type.267 = f32[2048,1536]{1,0:T(8,128)} convert(bf16[2048,1536]{1,0:T(8,128)(2,1)} %get-tuple-element.100) | non-fusion elementwise | flops 3145728 | bytes 18874368 | tf_op jit(solution)/shard_map/convert_element_type | solution.py:253
  652.5 6.6 convert_element_type.269
  659.0 6.3 convert_element_type.271
  665.3 61.3 %all-gather.12.cloned.1.call-done = bf16[16384,512]{1,0:T(8,128)(2,1)} async-done(((bf16[2048,512]{1,0:T(8,128)(2,1)}), bf16[16384,512]{1,0:T(8,128)(2,1)}) %all-gather.12.cloned.1.call-update) | async-done | bytes 16777232 | tf_op jit(solution)/shard_map/all_gather | solution.py:244
  726.6 10.7 %reduce_sum.167 = bf16[2048,512]{1,0:T(8,128)(2,1)} reduce(bf16[8,2048,512]{2,1,0:T(8,128)(2,1)} %bitcast.106, bf16[]{:T(256)} %constant.102.clone.1), dimensions={0}, to_apply=%region_21.22 | reduce | flops 7340032 | bytes 18874370 | tf_op jit(solution)/shard_map/reduce_sum | solution.py:244
  737.3 4.2 convert_element_type.253
  (240 shorter events, 45.4 us)
Async XLA Ops:
  7.2 61.0 %copy-start = (bf16[512,2048]{1,0:T(8,128)(2,1)S(1)}, bf16[512,2048]{1,0:T(8,128)(2,1)}, u32[]{:S(2)}) copy-start(bf16[512,2048]{1,0:T(8,128)(2,1)} %param.25) | copy-start | bytes 6291460
  7.2 33.1 %all-gather.6.cloned.1.call-start = ((), (), s32[]{:S(2)}) async-start(), calls=%async_computation.6 | async-start | bytes 1310720 | tf_op jit(solution)/shard_map/all_gather | solution.py:71
  7.9 106.2 %reduce-scatter.7.cloned.1.call-start = ((), (), s32[]{:S(2)}) async-start(), calls=%async_computation.7 | async-start | bytes 2621440 | tf_op jit(solution)/shard_map/reduce_scatter | solution.py:132
  8.6 55.5 %copy-start.57 = (f32[128]{0:T(128)}, f32[128]{0:T(128)S(1)}, u32[]{:S(2)}) copy-start(f32[128]{0:T(128)S(1)} %convert_element_type.217) | copy-start | bytes 1540
  11.2 49.0 %copy-start.55 = (f32[2048]{0:T(1024)}, f32[2048]{0:T(1024)S(1)}, u32[]{:S(2)}) copy-start(f32[2048]{0:T(1024)S(1)} %convert_element_type.210) | copy-start | bytes 24580
  11.7 28.5 %copy-start.16 = (f32[256,64]{1,0:T(8,128)}, f32[256,64]{1,0:T(8,128)S(1)}, u32[]{:S(2)}) copy-start(f32[256,64]{1,0:T(8,128)S(1)} %get-tuple-element.119) | copy-start | bytes 196612
  41.8 9.2 %copy-start.9 = (bf16[256,2048]{1,0:T(8,128)(2,1)S(1)}, bf16[256,2048]{1,0:T(8,128)(2,1)}, u32[]{:S(2)}) copy-start(bf16[256,2048]{1,0:T(8,128)(2,1)} %all-gather.6.cloned.1.call-done) | copy-start | bytes 3145732
  42.3 17.8 %copy-start.49 = (f32[256]{0:T(256)}, f32[256]{0:T(256)S(1)}, u32[]{:S(2)}) copy-start(f32[256]{0:T(256)S(1)} %get-tuple-element.121) | copy-start | bytes 3076
  50.9 9.3 %copy-start.22 = (bf16[2048,512]{1,0:T(8,128)(2,1)S(1)}, bf16[2048,512]{1,0:T(8,128)(2,1)}, u32[]{:S(2)}) copy-start(bf16[2048,512]{1,0:T(8,128)(2,1)} %param.20) | copy-start | bytes 6291460
  53.0 7.2 copy-start.53
  70.3 43.8 %copy-start.29 = (bf16[256,512]{1,0:T(8,128)(2,1)S(1)}, bf16[256,512]{1,0:T(8,128)(2,1)}, u32[]{:S(2)}) copy-start(bf16[256,512]{1,0:T(8,128)(2,1)} %param.15) | copy-start | bytes 786436
  70.3 46.1 %copy-start.51 = (bf16[2048]{0:T(1024)(128)(2,1)S(1)}, bf16[2048]{0:T(1024)(128)(2,1)}, u32[]{:S(2)}) copy-start(bf16[2048]{0:T(1024)(128)(2,1)} %param.26) | copy-start | bytes 12292
  70.3 73.1 %all-gather.8.cloned.1.call-start = ((), (), s32[]{:S(2)}) async-start(), calls=%async_computation.8 | async-start | bytes 1310720 | tf_op jit(solution)/shard_map/all_gather | solution.py:134
  115.9 88.7 %reduce-scatter.11.cloned.1.call-start = ((), (), s32[]{:S(2)}) async-start(), calls=%async_computation.10 | async-start | bytes 2621440 | tf_op jit(solution)/shard_map/reduce_scatter | solution.py:158
  143.4 7.3 slice-start.4
  145.6 5.1 copy-start.4
  145.6 5.1 slice-start.5
  145.6 7.1 slice-start.8
  150.7 7.1 slice-start.6
  152.7 5.2 slice-start.7
  161.1 84.8 %all-gather.10.cloned.1.call-start = ((), (), s32[]{:S(2)}) async-start(), calls=%async_computation.11 | async-start | bytes 1310720 | tf_op jit(solution)/shard_map/all_gather | solution.py:167
  219.5 62.4 %reduce-scatter.13.cloned.1.call-start = ((), (), s32[]{:S(2)}) async-start(), calls=%async_computation.12 | async-start | bytes 393216 | tf_op jit(solution)/shard_map/reduce_scatter | solution.py:208
  255.5 28.8 %reduce-scatter.15.cloned.1.call-start = ((), (), s32[]{:S(2)}) async-start(), calls=%async_computation.13 | async-start | bytes 393216 | tf_op jit(solution)/shard_map/reduce_scatter | solution.py:211
  257.8 53.8 %reduce-scatter.9.cloned.1.call-start = ((), (), s32[]{:S(2)}) async-start(), calls=%async_computation.9 | async-start | bytes 1310720 | tf_op jit(solution)/shard_map/reduce_scatter | solution.py:143
  267.9 6.0 copy-start.8
  267.9 6.0 copy-start.13
  273.8 66.4 %reduce-scatter.17.cloned.1.call-start = ((), (), s32[]{:S(2)}) async-start(), calls=%async_computation.14 | async-start | bytes 1310720 | tf_op jit(solution)/shard_map/reduce_scatter | solution.py:228
  274.3 3.6 copy-start.6
  276.3 3.8 copy-start.45
  276.3 4.0 copy-start.58
  277.8 5.1 copy-start.38
  277.8 5.1 copy-start.40
  280.0 3.7 copy-start.54
  288.2 6.1 copy-start.36
  288.2 345.9 %all-reduce.9.cloned.1.call-start = ((), (), s32[]{:S(2)}) async-start(), calls=%async_computation.16 | async-start | bytes 46137344 | tf_op jit(solution)/shard_map/psum | solution.py:247
  294.3 4.7 copy-start.34
  299.0 4.6 copy-start.28
  299.0 4.6 copy-start.31
  308.9 417.7 %all-gather.12.cloned.1.call-start = ((), (), s32[]{:S(2)}) async-start(), calls=%async_computation.15 | async-start | bytes 18874368 | tf_op jit(solution)/shard_map/all_gather | solution.py:244
  311.3 30.1 %copy-start.62 = (f32[128]{0:T(128)S(1)}, f32[128]{0:T(128)}, u32[]{:S(2)}) copy-start(f32[128]{0:T(128)} %get-tuple-element.73) | copy-start | bytes 1540
  311.3 30.1 %copy-start.63 = (f32[128]{0:T(128)S(1)}, f32[128]{0:T(128)}, u32[]{:S(2)}) copy-start(f32[128]{0:T(128)} %get-tuple-element.75) | copy-start | bytes 1540
  311.3 39.8 %copy-start.61 = (bf16[512]{0:T(512)(128)(2,1)S(1)}, bf16[512]{0:T(512)(128)(2,1)}, u32[]{:S(2)}) copy-start(bf16[512]{0:T(512)(128)(2,1)} %get-tuple-element.69) | copy-start | bytes 3076
  311.3 56.2 %copy-start.60 = (f32[256]{0:T(256)S(1)}, f32[256]{0:T(256)}, u32[]{:S(2)}) copy-start(f32[256]{0:T(256)} %get-tuple-element.120) | copy-start | bytes 3076
  639.2 13.2 %slice-start.2 = ((s8[6291456]{0:T(1024)(128)(4,1)}), s8[4194304]{0:T(1024)(128)(4,1)S(1)}, s32[]{:S(2)}) async-start(s8[6291456]{0:T(1024)(128)(4,1)} %bitcast.109), calls=%async_computation.19 | async-start | bytes 8388608
  641.9 10.5 %slice-start.3 = ((s8[6291456]{0:T(1024)(128)(4,1)}), s8[2097152]{0:T(1024)(128)(4,1)S(1)}, s32[]{:S(2)}) async-start(s8[6291456]{0:T(1024)(128)(4,1)} %bitcast.109), calls=%async_computation.20 | async-start | bytes 4194304
  641.9 17.1 %slice-start = ((s8[6291456]{0:T(1024)(128)(4,1)}), s8[4194304]{0:T(1024)(128)(4,1)S(1)}, s32[]{:S(2)}) async-start(s8[6291456]{0:T(1024)(128)(4,1)} %bitcast.107), calls=%async_computation.17 | async-start | bytes 8388608
  652.5 6.6 slice-start.1
  726.6 14.9 %copy-start.1 = (bf16[512,2048]{1,0:T(8,128)(2,1)S(1)}, bf16[512,2048]{1,0:T(8,128)(2,1)}, u32[]{:S(2)}) copy-start(bf16[512,2048]{1,0:T(8,128)(2,1)} %param.25) | copy-start | bytes 6291460
  (37 other events, 70.2 us)
Sparse Core Ops, SparseCore 0:
  9.6 30.6 all-gather.5
  70.4 43.6 reduce-scatter.6
  116.1 27.2 all-gather.7
  161.2 43.3 reduce-scatter.10
  219.6 26.2 all-gather.9
  255.7 11.1 reduce-scatter.12
  269.7 11.6 reduce-scatter.14
  284.3 27.1 reduce-scatter.8
  314.4 25.7 reduce-scatter.16
  346.1 287.9 all-reduce.8
  636.7 89.8 all-gather.11
